TPU v7x, 32 devices: a whole 2x2x4 slice. The times are simulated.
32 devices in a mesh: clip: 2 (over y), tm: 4 (over z), head: 2 (over x), sub: 2 (over core).
Axes of the slice: x: 2, y: 2, z: 4, core: 2. Of those that a mesh axis runs over, the one named last changes fastest.
Arguments:
- queries: bfloat16 [8, 256, 3072], P(('clip', 'tm'), None, ('head', 'sub')), parts along dimension 0, may hold values from -6 to 6, as said below
- keys: bfloat16 [8, 256, 3072], P(('clip', 'tm'), None, ('head', 'sub')), parts along dimension 0, may hold values from -6 to 6, as said below
- values: bfloat16 [8, 256, 3072], P(('clip', 'tm'), None, ('head', 'sub')), parts along dimension 0, may hold values from -6 to 6
- band_table: int32 [4, 4], replicated, may hold values from 0 to 3, as said below
- windows: int32 [7], replicated, may hold values from 1 to 128, as said below
- out_weight: bfloat16 [3072, 3072], P(('head', 'sub')), may hold values from -0.109375 to 0.109375
Outputs:
- mixed: bfloat16 [8, 256, 3072], P(('clip', 'tm'), ('head', 'sub')), parts along dimension 0
There are 2 independent parts, one for each index of `clip`. A program takes and returns all parts, laid end to end along the dimension named above; an argument that names none is the same for every part. Nothing has to cross between parts.
Inputs may be any that keep to these rules, and one draw needn't show every extreme that they name: `queries`: entries of normal law within the range; some rows may be aligned with some key rows. `keys`: entries of normal law within the range; some rows may be aligned with some query rows. `band_table`: Symmetric; 0 exactly on the diagonal; off the diagonal, for frames at distance d it is floor(log2 d) + 1 or one more, never above 6; the pair of frames 0 and 3 takes the one more (up to 6). windows[0] = 128; for k >= 1, windows[k] lies between max(1, 64 // 2**k) and max(that + 1, 128 // 2**k + 1) - 1.
All inputs are finite; a program needn't handle non-finite values.
Results may differ from a plain program's by a relative error of at most 0.015.
Values may be sent and summed in bfloat16 or wider, within the bound.
A program may use at most 64 MiB of HBM per device.

v0:
```python
import jax
import jax.numpy as jnp
from jax import lax
from jax.sharding import PartitionSpec as P

HEAD = 128


def local(queries, keys, values, band_table, windows, out_weight):
    frames, length, width = queries.shape
    heads = width // HEAD
    scale = HEAD ** (-0.5)
    here = lax.axis_index("tm") * frames
    query = queries[0].reshape(length, heads, HEAD)
    places = lax.iota(jnp.int32, length)
    gap = jnp.abs(places[:, None] - places[None, :])

    def absorb(carry, key_frame, value_frame, frame, usable):
        peak, total, numer = carry
        reach = windows[band_table[here, frame]]
        allowed = (gap <= reach)[None] & usable
        scores = (
            jnp.einsum(
                "phd,qhd->hpq",
                query,
                key_frame.reshape(length, heads, HEAD),
                preferred_element_type=jnp.float32,
            )
            * scale
        )
        masked = jnp.where(allowed, scores, jnp.float32(-1e30))
        top = jnp.maximum(peak, jnp.max(masked, axis=-1))
        weights = jnp.where(allowed, jnp.exp(scores - top[:, :, None]), jnp.float32(0.0))
        shrink = jnp.exp(peak - top)
        total = total * shrink + jnp.sum(weights, axis=-1)
        added = jnp.einsum(
            "hpq,qhd->phd",
            weights.astype(jnp.bfloat16),
            value_frame.reshape(length, heads, HEAD),
            preferred_element_type=jnp.float32,
        )
        numer = numer * jnp.transpose(shrink)[:, :, None] + added
        return (top, total, numer)

    carry = (
        jnp.full((heads, length), -1e30, jnp.float32),
        jnp.zeros((heads, length), jnp.float32),
        jnp.zeros((length, heads, HEAD), jnp.float32),
    )
    skipped = -1
    state = carry
    key_part = lax.all_gather(keys, "tm", axis=0, tiled=True)
    value_part = lax.all_gather(values, "tm", axis=0, tiled=True)

    def advance(inner, item):
        key_frame, value_frame, offset = item
        usable = jnp.abs(offset - here) > skipped
        return (absorb(inner, key_frame, value_frame, offset, usable), None)

    state, unused = lax.scan(
        advance, state, (key_part, value_part, lax.iota(jnp.int32, key_part.shape[0]))
    )
    carry = state
    peak, total, numer = carry
    attended = (
        (numer / jnp.transpose(total)[:, :, None]).astype(jnp.bfloat16).reshape(length, width)
    )
    mixed = lax.psum_scatter(
        jnp.dot(attended, out_weight, preferred_element_type=jnp.float32).astype(jnp.bfloat16),
        ("head", "sub"),
        scatter_dimension=0,
        tiled=True,
    )
    return mixed[None]


def solution(mesh):
    return jax.shard_map(
        local,
        mesh=mesh,
        in_specs=(
            P(("clip", "tm"), None, ("head", "sub")),
            P(("clip", "tm"), None, ("head", "sub")),
            P(("clip", "tm"), None, ("head", "sub")),
            P(),
            P(),
            P(("head", "sub"), None),
        ),
        out_specs=P(("clip", "tm"), ("head", "sub"), None),
        check_vma=False,
    )
```

profile of v0, /device:TPU:0, one launch (start us, length us, event | category | flops | bytes accessed | tf_op | source)
XLA Modules:
  0.0 169.9 jit_solution(7781933475861130219)
XLA Ops:
  6.5 0.0 copy-start
  6.5 0.0 all-gather.3.cloned.1.call-start
  6.5 0.7 all-gather.3.cloned.1.call-update
  7.3 0.0 all-gather.5.cloned.1.call-start
  7.3 0.7 all-gather.5.cloned.1.call-update
  8.0 0.0 reduce-scatter.2.cloned.1.call-start
  8.1 1.2 copy.17
  9.3 0.9 copy.19
  10.2 38.5 %all-gather.3.cloned.1.call-done = bf16[4,256,768]{2,1,0:T(8,128)(2,1)} async-done(((bf16[1,256,768]{2,1,0:T(8,128)(2,1)}), bf16[4,256,768]{2,1,0:T(8,128)(2,1)}) %all-gather.3.cloned.1.call-update) | async-done | bytes 1572880 | tf_op jit(solution)/shard_map/all_gather | solution.py:52
  48.7 37.5 %all-gather.5.cloned.1.call-done = bf16[4,256,768]{2,1,0:T(8,128)(2,1)} async-done(((bf16[1,256,768]{2,1,0:T(8,128)(2,1)}), bf16[4,256,768]{2,1,0:T(8,128)(2,1)}) %all-gather.5.cloned.1.call-update) | async-done | bytes 1572880 | tf_op jit(solution)/shard_map/all_gather | solution.py:53
  86.2 0.0 copy-done
  86.2 45.1 %while.17 = (s32[]{:T(128)}, f32[6,256]{1,0:T(8,128)S(1)}, f32[6,256]{1,0:T(8,128)S(1)}, f32[256,6,128]{0,2,1:T(8,128)S(1)}, s32[4]{0:T(128)S(1)}, /*index=5*/s3...) while((s32[]{:T(128)}, f32[6,256]{1,0:T(8,128)S(1)}, ...), condition=%wide.region_3.4_spmd.clone, body=%wide.region_0.3_spmd.clone.sunk | while | flops 205726720 | bytes 10977591 | solution.py:60
  86.2 0.6 dynamic_slice.39
  88.5 1.3 dynamic_slice.40
  91.7 0.6 dynamic_slice.41
  92.9 0.7 fusion.35
  93.6 1.2 constant_dynamic-slice_fusion.3
  94.8 0.2 copy.27
  94.9 1.5 fusion.36
  96.4 0.2 copy.28
  96.6 0.5 fusion.40
  97.1 0.3 fusion.38
  97.5 0.6 dynamic_slice.39
  99.7 1.3 dynamic_slice.40
  103.0 0.6 dynamic_slice.41
  104.2 0.7 fusion.35
  104.9 1.2 constant_dynamic-slice_fusion.3
  106.0 0.2 copy.27
  106.2 1.5 fusion.36
  107.7 0.2 copy.28
  107.9 0.5 fusion.40
  108.4 0.3 fusion.38
  108.7 0.6 dynamic_slice.39
  111.0 1.3 dynamic_slice.40
  114.2 0.6 dynamic_slice.41
  115.4 0.7 fusion.35
  116.2 1.2 constant_dynamic-slice_fusion.3
  117.3 0.2 copy.27
  117.5 1.5 fusion.36
  119.0 0.2 copy.28
  119.2 0.5 fusion.40
  119.7 0.3 fusion.38
  120.0 0.6 dynamic_slice.39
  122.3 1.3 dynamic_slice.40
  125.5 0.6 dynamic_slice.41
  126.7 0.7 fusion.35
  127.4 1.2 constant_dynamic-slice_fusion.3
  128.6 0.2 copy.27
  128.8 1.4 fusion.36
  130.3 0.2 copy.28
  130.4 0.5 fusion.40
  131.0 0.3 fusion.38
  131.3 0.1 divide_convert_fusion
  131.4 4.9 %convolution_convert_fusion = bf16[256,3072]{1,0:T(8,128)(2,1)} fusion(bf16[256,768]{0,1:T(8,128)(2,1)S(1)} %bitcast.62, bf16[768,3072]{1,0:T(8,128)(2,1)} %param.13), kind=kOutput, calls=%fused_computation.25 | convolution fusion | flops 1208745984 | bytes 6684672 | tf_op jit(solution)/shard_map/dot_general | solution.py:69
  136.3 0.0 reduce-scatter.2.cloned.1.call-update
  136.3 27.0 %reduce-scatter.2.cloned.1.call-done = bf16[64,3072]{1,0:T(8,128)(2,1)} async-done(((bf16[256,3072]{1,0:T(8,128)(2,1)}), bf16[64,3072]{1,0:T(8,128)(2,1)}) %reduce-scatter.2.cloned.1.call-update) | async-done | bytes 393232 | tf_op jit(solution)/shard_map/reduce_scatter | solution.py:68
  (16 shorter events, 0.1 us)
Async XLA Ops:
  6.5 79.6 %copy-start = (s32[7]{0:T(128)S(1)}, s32[7]{0:T(128)}, u32[]{:S(2)}) copy-start(s32[7]{0:T(128)} %param.12) | copy-start | bytes 88
  6.5 42.1 %all-gather.3.cloned.1.call-start = ((), (), s32[]{:S(2)}) async-start(), calls=%async_computation.1 | async-start | bytes 1966080 | tf_op jit(solution)/shard_map/all_gather | solution.py:52
  7.3 78.9 %all-gather.5.cloned.1.call-start = ((), (), s32[]{:S(2)}) async-start(), calls=%async_computation.2 | async-start | bytes 1966080 | tf_op jit(solution)/shard_map/all_gather | solution.py:53
  8.0 155.3 %reduce-scatter.2.cloned.1.call-start = ((), (), s32[]{:S(2)}) async-start(), calls=%async_computation.3 | async-start | bytes 1966080 | tf_op jit(solution)/shard_map/reduce_scatter | solution.py:68
Sparse Core Ops, SparseCore 0:
  8.9 39.7 all-gather.2
  50.2 35.8 all-gather.4
  136.4 26.8 reduce-scatter.1
where the time goes:
time: 171 us; the launch traced here: 170 us
  waiting for transfers between devices  104 us (61%)
  local copies, waits for them, and re-layouts  18.4 us (11%)
  loops' own time  16.9 us (10%)
  between operations  13.2 us (8%)
  matrix products  12.8 us (7%)
  other arithmetic  4.12 us (2%)
    all_gather x1, waiting for transfers between devices, local(): key_part = lax.all_gather(keys, 'tm', axis=0, tiled=True)  38.5 us
    all_gather x1, waiting for transfers between devices, local(): value_part = lax.all_gather(values, 'tm', axis=0, tiled=True)  37.5 us
    reduce_scatter x1, waiting for transfers between devices, local(): lax.psum_scatter(jnp.dot(attended, out_weight, preferred_element_type=jnp...  27 us
    another operation x1, loops' own time, local(): lax.scan(advance, state, (key_part, value_part, lax.iota(jnp.int32, key_p...  16.9 us
    dynamic_slice x16, local copies, waits for them, and re-layouts, local(): lax.scan(advance, state, (key_part, value_part, lax.iota(jnp.int32, key_p...  8.4 us
    dynamic_slice x8, local copies, waits for them, and re-layouts, absorb(): reach = windows[band_table[here, frame]]  7.86 us
    dot_general x4, matrix products, absorb(): jnp.einsum('phd,qhd->hpq', query, key_frame.reshape(length, heads, HEAD),...  5.81 us
    dot_general x1, matrix products, local(): jnp.dot(attended, out_weight, preferred_element_type=jnp.float32)  4.92 us
  transfers between devices with their start and end apart: 3, of which 3 were waited for; matrix products, arithmetic and copies ran while one was open for 1% of the time, Pallas kernels for 0%

commit v1 on v0

--- a/solution.py
+++ b/solution.py
@@ -1,9 +1,27 @@
+import functools
 import jax
 import jax.numpy as jnp
 from jax import lax
 from jax.sharding import PartitionSpec as P
 
 HEAD = 128
+
+
+def order_ports(xin, chip_axis):
+    amount_of = lax.axis_size(chip_axis)
+    frame_out = range(amount_of)
+    row_out = map(lambda w: (w, (w + 1) % amount_of), frame_out)
+    a_next = [None] * amount_of
+    a_next[amount_of - 1] = xin
+    crops = list(row_out)
+    for hop_no in range(amount_of - 2, -1, -1):
+        a_next[hop_no] = lax.ppermute(a_next[hop_no + 1], perm=crops, axis_name=chip_axis)
+    v1 = jnp.concatenate(a_next, axis=0)
+    oldest = (lax.axis_index(chip_axis) + 1) * xin.shape[0]
+    return jnp.roll(v1, oldest, axis=0)
+
+
+store_layers_all = functools.partial(order_ports, chip_axis="tm")
 
 
 def local(queries, keys, values, band_table, windows, out_weight):
@@ -50,7 +68,7 @@
     skipped = -1
     state = carry
     key_part = lax.all_gather(keys, "tm", axis=0, tiled=True)
-    value_part = lax.all_gather(values, "tm", axis=0, tiled=True)
+    value_part = store_layers_all(values)
 
     def advance(inner, item):
         key_frame, value_frame, offset = item

time: 171 us -> 149 us (0.87)
  waiting for transfers between devices: 104 us -> 75 us
  starting transfers between devices: 0.08 us -> 8.3 us
  local copies, waits for them, and re-layouts: 18.4 us -> 22.8 us
  matrix products: 12.8 us -> 8.84 us
    ppermute x0 -> x3, waiting for transfers between devices: none -> 47.8 us  [order_ports(): lax.ppermute(a_next[hop_no + 1], perm=crops, axis_name=chip_axis)]
    all_gather x1, waiting for transfers between devices: 38.5 us -> 0.01 us  [local(): key_part = lax.all_gather(keys, 'tm', axis=0, tiled=True)]
    all_gather x1 -> x0, waiting for transfers between devices: 37.5 us -> none  [local(): value_part = lax.all_gather(values, 'tm', axis=0, tiled=True)]
    ppermute x0 -> x3, starting transfers between devices: none -> 8.26 us  [order_ports(): lax.ppermute(a_next[hop_no + 1], perm=crops, axis_name=chip_axis)]
    dot_general x4, matrix products: 5.81 us -> 1.83 us  [absorb(): jnp.einsum('phd,qhd->hpq', query, key_frame.reshape(length, heads, HEAD),...]
    dynamic_slice x16, local copies, waits for them, and re-layouts: 8.4 us -> 11.3 us  [local(): lax.scan(advance, state, (key_part, value_part, lax.iota(jnp.int32, key_p...]
  transfers between devices with their start and end apart: 3 -> 5, of which waited for: 3 -> 4; matrix products, arithmetic and copies ran while one was open for 1% -> 3% of each run, Pallas kernels for 0% -> 0%
where the time goes in v1:
time: 149 us; the launch traced here: 148 us
  waiting for transfers between devices  75 us (50%)
  local copies, waits for them, and re-layouts  22.8 us (15%)
  loops' own time  16.1 us (11%)
  between operations  13.5 us (9%)
  matrix products  8.84 us (6%)
  starting transfers between devices  8.3 us (6%)
  other arithmetic  3.85 us (3%)
    ppermute x3, waiting for transfers between devices, order_ports(): lax.ppermute(a_next[hop_no + 1], perm=crops, axis_name=chip_axis)  47.8 us
    reduce_scatter x1, waiting for transfers between devices, local(): lax.psum_scatter(jnp.dot(attended, out_weight, preferred_element_type=jnp...  26.5 us
    another operation x1, loops' own time, local(): lax.scan(advance, state, (key_part, value_part, lax.iota(jnp.int32, key_p...  16.1 us
    dynamic_slice x16, local copies, waits for them, and re-layouts, local(): lax.scan(advance, state, (key_part, value_part, lax.iota(jnp.int32, key_p...  11.3 us
    ppermute x3, starting transfers between devices, order_ports(): lax.ppermute(a_next[hop_no + 1], perm=crops, axis_name=chip_axis)  8.26 us
    dynamic_slice x8, local copies, waits for them, and re-layouts, absorb(): reach = windows[band_table[here, frame]]  7.46 us
    dot_general x1, matrix products, local(): jnp.dot(attended, out_weight, preferred_element_type=jnp.float32)  4.92 us
  transfers between devices with their start and end apart: 5, of which 4 were waited for; matrix products, arithmetic and copies ran while one was open for 3% of the time, Pallas kernels for 0%

profile of v1, /device:TPU:0, one launch (start us, length us, event | category | flops | bytes accessed | tf_op | source)
XLA Modules:
  0.0 148.4 jit_solution(16508331547041042653)
XLA Ops:
  6.5 0.0 all-gather.2.cloned.1.call-start
  6.5 0.7 all-gather.2.cloned.1.call-update
  7.3 0.0 reduce-scatter.2.cloned.1.call-start
  7.3 1.2 copy.22
  8.5 3.1 %collective-permute-start = (bf16[1,256,768]{1,2,0:T(8,128)(2,1)S(1)}, bf16[1,256,768]{1,2,0:T(8,128)(2,1)S(1)}, u32[]{:S(2)}, u32[]{:S(2)}) collective-permute-start(bf16[1,256,768]{1,2,0:T(8,128)(2,1)S(1)} %copy.22), channel_id=1, source_target_pairs={{0,4},{4,8},{8,12},{12,0},{1,5},{5,9},{9,13},{13,1},{2,6},{6,10},{... | collective-permute-start | bytes 1179656 | tf_op jit(solution)/shard_map/ppermute | solution.py:18
  11.6 11.2 %collective-permute-done = bf16[1,256,768]{1,2,0:T(8,128)(2,1)S(1)} collective-permute-done((bf16[1,256,768]{1,2,0:T(8,128)(2,1)S(1)}, bf16[1,256,768]{1,2,0:T(8,128)(2,1)S(1)}, u32[]{:S(2)}, u32[]{:S(2)}) %collective-permute-start) | collective-permute-done | bytes 393248 | tf_op jit(solution)/shard_map/ppermute | solution.py:18
  22.8 0.0 collective-permute-start.1
  22.8 21.7 %collective-permute-done.1 = bf16[1,256,768]{1,2,0:T(8,128)(2,1)S(1)} collective-permute-done((bf16[1,256,768]{1,2,0:T(8,128)(2,1)S(1)}, bf16[1,256,768]{1,2,0:T(8,128)(2,1)S(1)}, u32[]{:S(2)}, u32[]{:S(2)}) %collective-permute-start.1) | collective-permute-done | bytes 393248 | tf_op jit(solution)/shard_map/ppermute | solution.py:18
  44.5 5.2 %collective-permute-start.2 = (bf16[1,256,768]{1,2,0:T(8,128)(2,1)S(1)}, bf16[1,256,768]{1,2,0:T(8,128)(2,1)S(1)}, u32[]{:S(2)}, u32[]{:S(2)}) collective-permute-start(bf16[1,256,768]{1,2,0:T(8,128)(2,1)S(1)} %collective-permute-done.1), channel_id=1, source_target_pairs={{0,4},{4,8},{8,12},{12,0},{1,5},{5,9},{9,13},{13,1},{2,6},{6,10},{... | collective-permute-start | bytes 1179656 | tf_op jit(solution)/shard_map/ppermute | solution.py:18
  49.6 1.2 copy.21
  50.8 0.2 copy.26
  51.0 14.9 %collective-permute-done.2 = bf16[1,256,768]{1,2,0:T(8,128)(2,1)S(1)} collective-permute-done((bf16[1,256,768]{1,2,0:T(8,128)(2,1)S(1)}, bf16[1,256,768]{1,2,0:T(8,128)(2,1)S(1)}, u32[]{:S(2)}, u32[]{:S(2)}) %collective-permute-start.2) | collective-permute-done | bytes 393248 | tf_op jit(solution)/shard_map/ppermute | solution.py:18
  66.0 0.0 copy-start
  66.2 1.3 constant_dynamic-slice_fusion.2
  67.5 0.0 all-gather.2.cloned.1.call-done
  67.5 0.0 copy-done
  67.5 42.5 %while.17 = (s32[]{:T(128)}, f32[6,256]{1,0:T(8,128)S(1)}, f32[6,256]{1,0:T(8,128)S(1)}, f32[256,6,128]{0,2,1:T(8,128)S(1)}, s32[4]{0:T(128)S(1)}, /*index=5*/s3...) while((s32[]{:T(128)}, f32[6,256]{1,0:T(8,128)S(1)}, ...), condition=%wide.region_3.4_spmd.clone, body=%wide.region_0.3_spmd.clone.sunk | while | flops 205726720 | bytes 10191163 | solution.py:78
  67.5 0.6 dynamic_slice.47
  69.7 1.3 dynamic_slice.48
  72.7 0.6 dynamic_slice.49
  73.9 0.6 fusion.35
  74.5 1.0 constant_dynamic-slice_fusion.5
  75.5 0.2 copy.31
  75.7 0.5 fusion.36
  76.2 1.0 constant_dynamic-slice_fusion.6
  77.2 0.5 fusion.40
  77.8 0.3 fusion.38
  78.1 0.6 dynamic_slice.47
  80.4 1.3 dynamic_slice.48
  83.3 0.6 dynamic_slice.49
  84.5 0.6 fusion.35
  85.1 1.0 constant_dynamic-slice_fusion.5
  86.2 0.2 copy.31
  86.3 0.5 fusion.36
  86.8 1.0 constant_dynamic-slice_fusion.6
  87.9 0.5 fusion.40
  88.4 0.3 fusion.38
  88.7 0.6 dynamic_slice.47
  91.0 1.3 dynamic_slice.48
  94.0 0.6 dynamic_slice.49
  95.1 0.6 fusion.35
  95.8 1.0 constant_dynamic-slice_fusion.5
  96.8 0.2 copy.31
  97.0 0.5 fusion.36
  97.4 1.0 constant_dynamic-slice_fusion.6
  98.5 0.5 fusion.40
  99.0 0.3 fusion.38
  99.3 0.6 dynamic_slice.47
  101.6 1.3 dynamic_slice.48
  104.6 0.6 dynamic_slice.49
  105.7 0.6 fusion.35
  106.4 1.0 constant_dynamic-slice_fusion.5
  107.4 0.2 copy.31
  107.6 0.5 fusion.36
  108.1 1.0 constant_dynamic-slice_fusion.6
  109.1 0.5 fusion.40
  109.6 0.3 fusion.38
  110.0 0.1 divide_convert_fusion
  110.0 4.9 %convolution_convert_fusion = bf16[256,3072]{1,0:T(8,128)(2,1)} fusion(bf16[256,768]{0,1:T(8,128)(2,1)S(1)} %bitcast.62, bf16[768,3072]{1,0:T(8,128)(2,1)} %param.13), kind=kOutput, calls=%fused_computation.25 | convolution fusion | flops 1208745984 | bytes 6684672 | tf_op jit(solution)/shard_map/dot_general | solution.py:87
  115.0 0.0 reduce-scatter.2.cloned.1.call-update
  115.0 26.5 %reduce-scatter.2.cloned.1.call-done = bf16[64,3072]{1,0:T(8,128)(2,1)} async-done(((bf16[256,3072]{1,0:T(8,128)(2,1)}), bf16[64,3072]{1,0:T(8,128)(2,1)}) %reduce-scatter.2.cloned.1.call-update) | async-done | bytes 393232 | tf_op jit(solution)/shard_map/reduce_scatter | solution.py:86
  (24 shorter events, 0.3 us)
Async XLA Ops:
  6.5 60.9 %all-gather.2.cloned.1.call-start = ((), (), s32[]{:S(2)}) async-start(), calls=%async_computation.1 | async-start | bytes 1966080 | tf_op jit(solution)/shard_map/all_gather | solution.py:70
  7.3 134.3 %reduce-scatter.2.cloned.1.call-start = ((), (), s32[]{:S(2)}) async-start(), calls=%async_computation.2 | async-start | bytes 1966080 | tf_op jit(solution)/shard_map/reduce_scatter | solution.py:86
  8.5 14.3 %collective-permute-start = (bf16[1,256,768]{1,2,0:T(8,128)(2,1)S(1)}, bf16[1,256,768]{1,2,0:T(8,128)(2,1)S(1)}, u32[]{:S(2)}, u32[]{:S(2)}) collective-permute-start(bf16[1,256,768]{1,2,0:T(8,128)(2,1)S(1)} %copy.22), channel_id=1, source_target_pairs={{0,4},{4,8},{8,12},{12,0},{1,5},{5,9},{9,13},{13,1},{2,6},{6,10},{... | collective-permute-start | bytes 1179656 | tf_op jit(solution)/shard_map/ppermute | solution.py:18
  22.8 21.7 %collective-permute-start.1 = (bf16[1,256,768]{1,2,0:T(8,128)(2,1)S(1)}, bf16[1,256,768]{1,2,0:T(8,128)(2,1)S(1)}, u32[]{:S(2)}, u32[]{:S(2)}) collective-permute-start(bf16[1,256,768]{1,2,0:T(8,128)(2,1)S(1)} %collective-permute-done), channel_id=1, source_target_pairs={{0,4},{4,8},{8,12},{12,0},{1,5},{5,9},{9,13},{13,1},{2,6},{6,10},{... | collective-permute-start | bytes 1179656 | tf_op jit(solution)/shard_map/ppermute | solution.py:18
  44.5 21.5 %collective-permute-start.2 = (bf16[1,256,768]{1,2,0:T(8,128)(2,1)S(1)}, bf16[1,256,768]{1,2,0:T(8,128)(2,1)S(1)}, u32[]{:S(2)}, u32[]{:S(2)}) collective-permute-start(bf16[1,256,768]{1,2,0:T(8,128)(2,1)S(1)} %collective-permute-done.1), channel_id=1, source_target_pairs={{0,4},{4,8},{8,12},{12,0},{1,5},{5,9},{9,13},{13,1},{2,6},{6,10},{... | collective-permute-start | bytes 1179656 | tf_op jit(solution)/shard_map/ppermute | solution.py:18
  66.0 1.4 copy-start
Sparse Core Ops, SparseCore 0:
  8.9 51.3 all-gather.1
  115.1 26.3 reduce-scatter.1
